TPU v7x, 32 devices: a whole 2x2x4 slice. The times are simulated.
32 devices in a mesh: pair: 8 (over z, core), cd: 4 (over y, x).
Axes of the slice: x: 2, y: 2, z: 4, core: 2. Of those that a mesh axis runs over, the one named last changes fastest.
Arguments:
- amplitudes: float32 [2048, 4096], P('pair', 'cd'), may hold values from -6 to 6
- integrals: float32 [4096, 256], P(('cd', 'pair')), may hold values from -0.09375 to 0.09375
- keep_tiles: int32 [32, 2], replicated, may hold values from 0 to 1, as said below
Outputs:
- ladder: float32 [2048, 256], P(('pair', 'cd'))
Inputs may be any that keep to these rules, and one draw needn't show every extreme that they name: `keep_tiles`: each entry is 0 (tile screened out) or 1 (tile kept); each tile row keeps at most one tile, and some tile row keeps one.
All inputs are finite; a program needn't handle non-finite values.
Results may differ from a plain program's by a relative error of at most 0.000071.
Values sent between devices are 32-bit elements; how exact they have to be, the bound alone decides.
A program may use at most 64 MiB of HBM per device.

v0:
```python
import functools

import jax
import jax.numpy as jnp
from jax import lax
from jax.experimental import pallas as pl
from jax.experimental.pallas import tpu as pltpu
from jax.sharding import PartitionSpec as P

TILE = 128
CORES = 2
CHUNKS = 1
MESH = pl.DeviceIdType.MESH


def flip(i, bits):
    b = 1
    out = i
    while b <= bits:
        if bits & b:
            out = out + b - 2 * b * (lax.rem(lax.div(i, b), 2))
        b *= 2
    return out


def split(x):
    hi = x.astype(jnp.bfloat16)
    lo = (x - hi.astype(jnp.float32)).astype(jnp.bfloat16)
    return hi, lo


def dot3(a_hi, a_lo, b_hi, b_lo):
    d = functools.partial(
        lax.dot_general, dimension_numbers=(((1,), (1,)), ((), ())), preferred_element_type=jnp.float32)
    return d(a_hi, b_hi) + (d(a_lo, b_hi) + d(a_hi, b_lo))


def kernel(pairs, cds, flags_hbm, v_hbm, a_hbm, out_ref, flags, v, a, tiles, a_hi, a_lo, acc, land,
           load_sem, ssem, rsem, psend, precv, rs_send, rs_recv):
    nz = pairs // CORES
    me = lax.axis_index("pair")
    cd = lax.axis_index("cd")
    z = lax.div(me, CORES)
    core = lax.rem(me, CORES)
    partner = me + 1 - 2 * core
    blocks = v.shape[1] // TILE
    part = TILE // CHUNKS
    rows = out_ref.shape[0]

    def valid(d, s):
        return z - s >= 0 if d == 0 else z + s < nz

    load_v = pltpu.make_async_copy(v_hbm, v, load_sem.at[0])
    load_v.start()
    load_f = pltpu.make_async_copy(flags_hbm, flags, load_sem.at[2])
    load_f.start()
    load_a = pltpu.make_async_copy(a_hbm, a, load_sem.at[1])
    load_a.start()

    has_next = (z + 1 < nz, z > 0)
    neighbour = (me + CORES, me - CORES)

    barrier = pltpu.get_barrier_semaphore()
    for d in range(2):
        for s in range(nz - 1):
            far = me + (s + 1) * CORES if d == 0 else me - (s + 1) * CORES
            @pl.when(valid(1 - d, s + 1))
            def _():
                pl.semaphore_signal(barrier, inc=1, device_id={"pair": far}, device_id_type=MESH)
    for j in range(1, cds):
        pl.semaphore_signal(barrier, inc=1, device_id={"cd": flip(cd, j)}, device_id_type=MESH)
    pl.semaphore_signal(barrier, inc=1, device_id={"pair": partner}, device_id_type=MESH)

    load_f.wait()
    load_v.wait()
    row_block = cd * pairs + me
    own = v[:, :TILE] * flags[0, row_block].astype(jnp.float32)
    for m in range(1, blocks):
        own = own + v[:, m * TILE:(m + 1) * TILE] * flags[m, row_block].astype(jnp.float32)
    tiles[me] = own.T

    greeted = cds + nz - 1
    pl.semaphore_wait(barrier, greeted)

    def stream(d, s, c, k):
        r = pl.ds(c * part, part)
        far = me + (s + 1) * CORES if d == 0 else me - (s + 1) * CORES
        return pltpu.make_async_remote_copy(
            src_ref=tiles.at[k, r], dst_ref=tiles.at[k, r],
            send_sem=ssem.at[d, s, c], recv_sem=rsem.at[d, s, c],
            device_id={"pair": far}, device_id_type=MESH)

    def exchange(d, s, c, k):
        r = pl.ds(c * part, part)
        return pltpu.make_async_remote_copy(
            src_ref=tiles.at[k, r], dst_ref=tiles.at[k, r],
            send_sem=psend.at[d, s, c], recv_sem=precv.at[d, s, c],
            device_id={"pair": partner}, device_id_type=MESH)

    def origin(d, s):
        return z - s if d == 0 else z + s

    for s in range(nz - 2, -1, -1):
        for c in range(CHUNKS):
            for d in (1, 0):
                @pl.when(valid(1 - d, s + 1))
                def _():
                    stream(d, s, c, me).start()
    for c in range(CHUNKS):
        exchange(0, 0, c, me).start()

    load_a.wait()
    hi, lo = split(a[...])
    a_hi[...] = hi
    a_lo[...] = lo

    def compute(d, s, c):
        chip = origin(d, s)
        exchange(d, s, c, chip * CORES + 1 - core).wait_recv()
        halves = []
        for i in range(CORES):
            k = chip * CORES + i
            t = tiles[k, c * part:(c + 1) * part]
            g = cd * pairs + k
            halves.append(jnp.concatenate(
                [t * flags[m, g].astype(jnp.float32) for m in range(blocks)], axis=0))
        b_hi, b_lo = split(jnp.concatenate(halves, axis=1))
        cols = pl.ds(pl.multiple_of(chip * (CORES * TILE), CORES * TILE), CORES * TILE)
        prod = dot3(a_hi[:, cols], a_lo[:, cols], b_hi, b_lo)
        if s == 0:
            acc[c] = prod
        else:
            acc[c] += prod

    def compute_step(s, c):
        if s == 0:
            compute(0, 0, c)
        else:
            for d in range(2):
                @pl.when(valid(d, s))
                def _():
                    compute(d, s, c)

    for s in range(1, nz):
        for c in range(CHUNKS):
            for d in range(2):
                @pl.when(valid(d, s))
                def _():
                    k = origin(d, s) * CORES + core
                    stream(d, s - 1, c, k).wait_recv()
                    exchange(d, s, c, k).start()
            compute_step(s - 1, c)

    def scatter(j, c):
        q = flip(cd, j)
        return pltpu.make_async_remote_copy(
            src_ref=acc.at[c, pl.ds(pl.multiple_of(q * rows, rows), rows)], dst_ref=land.at[j - 1, c],
            send_sem=rs_send.at[j - 1, c], recv_sem=rs_recv.at[j - 1, c],
            device_id={"cd": q}, device_id_type=MESH)

    for c in range(CHUNKS):
        compute_step(nz - 1, c)
        for j in range(cds - 1, 0, -1):
            scatter(j, c).start()

    for c in range(CHUNKS):
        exchange(0, 0, c, me).wait_send()
        for d in range(2):
            for s in range(nz - 1):
                @pl.when(valid(1 - d, s + 1))
                def _():
                    stream(d, s, c, me).wait_send()
    for s in range(1, nz):
        for d in range(2):
            @pl.when(valid(d, s))
            def _():
                k = origin(d, s) * CORES + core
                for c in range(CHUNKS):
                    exchange(d, s, c, k).wait_send()

    totals = []
    for c in range(CHUNKS):
        total = acc[c, pl.ds(pl.multiple_of(cd * rows, rows), rows)]
        for j in range(1, cds):
            scatter(j, c).wait_recv()
            total = total + land[j - 1, c]
        totals.append(total)
    for m in range(blocks):
        out_ref[:, m * TILE:(m + 1) * TILE] = jnp.concatenate(
            [t[:, m * part:(m + 1) * part] for t in totals], axis=1)
    for c in range(CHUNKS):
        for j in range(1, cds):
            scatter(j, c).wait_send()


def solution(mesh):
    pairs, cds = mesh.shape["pair"], mesh.shape["cd"]
    nz = pairs // CORES

    def local(amplitudes, integrals, keep_tiles):
        n, depth = amplitudes.shape
        ab = integrals.shape[1]
        rows = n // cds
        return pl.pallas_call(
            functools.partial(kernel, pairs, cds),
            out_shape=pltpu.VMEM((rows, ab), jnp.float32),
            in_specs=[
                pl.BlockSpec(memory_space=pl.ANY),
                pl.BlockSpec(memory_space=pl.ANY),
                pl.BlockSpec(memory_space=pl.ANY),
            ],
            out_specs=pl.BlockSpec(memory_space=pltpu.VMEM),
            scratch_shapes=[
                pltpu.SMEM(keep_tiles.shape[::-1], jnp.int32),
                pltpu.VMEM(integrals.shape, jnp.float32),
                pltpu.VMEM((n, depth), jnp.float32),
                pltpu.VMEM((pairs, TILE, TILE), jnp.float32),
                pltpu.VMEM((n, depth), jnp.bfloat16),
                pltpu.VMEM((n, depth), jnp.bfloat16),
                pltpu.VMEM((CHUNKS, n, ab // CHUNKS), jnp.float32),
                pltpu.VMEM((cds - 1, CHUNKS, rows, ab // CHUNKS), jnp.float32),
                pltpu.SemaphoreType.DMA((3,)),
                pltpu.SemaphoreType.DMA((2, nz, CHUNKS)),
                pltpu.SemaphoreType.DMA((2, nz, CHUNKS)),
                pltpu.SemaphoreType.DMA((2, nz, CHUNKS)),
                pltpu.SemaphoreType.DMA((2, nz, CHUNKS)),
                pltpu.SemaphoreType.DMA((cds - 1, CHUNKS)),
                pltpu.SemaphoreType.DMA((cds - 1, CHUNKS)),
            ],
            compiler_params=pltpu.CompilerParams(collective_id=0, has_side_effects=True),
        )(keep_tiles.T, integrals, amplitudes)

    placed = (P("pair", "cd"), P(("cd", "pair"), None), P())
    return jax.shard_map(
        local, mesh=mesh, in_specs=placed, out_specs=P(("pair", "cd"), None), check_vma=False
    )
```

profile of v0, /device:TPU:0, one launch (start us, length us, event | category | flops | bytes accessed | tf_op | source)
XLA Modules:
  0.0 19.1 jit_solution(11863778521104568246)
XLA Ops:
  0.0 18.4 %shard_map.37 = f32[64,256]{1,0:T(8,128)S(1)} custom-call(s32[2,32]{1,0:T(2,128)} %bitcast.1, f32[128,256]{1,0:T(8,128)} %v_hbm.1, f32[256,1024]{1,0:T(8,128)} %a_hbm.1), custom_call_target="tpu_custom_call" | custom-call | tf_op jit(solution)/shard_map/pallas_call | solution.py:204
  18.4 0.6 %copy.5 = f32[64,256]{1,0:T(8,128)} copy(f32[64,256]{1,0:T(8,128)S(1)} %shard_map.37) | data formatting | bytes 131072
where the time goes:
time: 19.2 us; the launch traced here: 19.1 us
  Pallas kernels  18.4 us (96%)
  local copies, waits for them, and re-layouts  0.63 us (3%)
    pallas_call x1, Pallas kernels, local(): pl.pallas_call(functools.partial(kernel, pairs, cds), out_shape=pltpu.VME...  18.4 us
    unnamed x1, local copies, waits for them, and re-layouts  0.63 us

commit v1 on v0

v1 whole, which is shorter than its diff:
```python
import functools

import jax
import jax.numpy as jnp
from jax import lax
from jax.experimental import pallas as pl
from jax.experimental.pallas import tpu as pltpu
from jax.sharding import PartitionSpec as P

TILE = 128
CORES = 2
HOLD = 1000
MESH = pl.DeviceIdType.MESH


def split(x):
    hi = x.astype(jnp.bfloat16)
    lo = (x - hi.astype(jnp.float32)).astype(jnp.bfloat16)
    return hi, lo


def kernel(pairs, cds, flags_hbm, v_hbm, a_hbm, out_ref, flags, v, a, tiles, a_cat, acc, land,
           load_sem, ssem, rsem, psend, precv, rs_send, rs_recv, zready, pready, cready, cgo):
    nz = pairs // CORES
    width = CORES * TILE
    me = lax.axis_index("pair")
    cd = lax.axis_index("cd")
    z = lax.div(me, CORES)
    core = lax.rem(me, CORES)
    partner = me + 1 - 2 * core
    blocks = v.shape[1] // TILE
    rows = out_ref.shape[0]

    load_v = pltpu.make_async_copy(v_hbm, v, load_sem.at[0])
    load_v.start()
    load_f = pltpu.make_async_copy(flags_hbm, flags, load_sem.at[2])
    load_f.start()
    load_a = pltpu.make_async_copy(a_hbm, a, load_sem.at[1])
    load_a.start()

    def signal(sem, axis, to):
        pl.semaphore_signal(sem, inc=1, device_id={axis: to}, device_id_type=MESH)

    barrier = pltpu.get_barrier_semaphore()
    for i in range(1, nz):
        @pl.when(z + i < nz)
        def _():
            signal(barrier, "pair", me + i * CORES)
    @pl.when(cd == 0)
    def _():
        for i in range(1, cds):
            signal(barrier, "cd", i)
    @pl.when(core == 1)
    def _():
        signal(barrier, "pair", partner)
    greeted = z + jnp.where(cd > 0, 1, 0) + 1 - core
    @pl.when(greeted > 0)
    def _():
        pl.semaphore_wait(barrier, greeted)
    for i in range(1, nz):
        @pl.when(z >= i)
        def _():
            signal(zready.at[z], "pair", me - i * CORES)
    @pl.when(core == 0)
    def _():
        signal(pready, "pair", partner)
    @pl.when(cd > 0)
    def _():
        signal(cready, "cd", 0)

    load_f.wait()
    load_v.wait()
    row_block = cd * pairs + me
    own = v[:, :TILE] * flags[0, row_block].astype(jnp.float32)
    for m in range(1, blocks):
        own = own + v[:, m * TILE:(m + 1) * TILE] * flags[m, row_block].astype(jnp.float32)
    tiles[me] = own.T

    def send(chip):
        return pltpu.make_async_remote_copy(
            src_ref=tiles.at[me], dst_ref=tiles.at[me], send_sem=ssem.at[chip], recv_sem=rsem.at[z],
            device_id={"pair": chip * CORES + core}, device_id_type=MESH)

    def arrival(chip):
        k = chip * CORES + core
        return pltpu.make_async_remote_copy(
            src_ref=tiles.at[k], dst_ref=tiles.at[k], send_sem=ssem.at[chip], recv_sem=rsem.at[chip],
            device_id={"pair": k}, device_id_type=MESH)

    def exchange(chip, side):
        k = chip * CORES + side
        return pltpu.make_async_remote_copy(
            src_ref=tiles.at[k], dst_ref=tiles.at[k], send_sem=psend.at[chip], recv_sem=precv.at[chip],
            device_id={"pair": partner}, device_id_type=MESH)

    @pl.when(z > 0)
    def _():
        send(0).start()
    @pl.when(core == 1)
    def _():
        pl.semaphore_wait(pready, 1)
    exchange(z, core).start()
    for i in range(1, nz):
        @pl.when(z + i < nz)
        def _():
            pl.semaphore_wait(zready.at[z + i], 1)
            send(z + i).start()
    exchange(z, 1 - core).wait_recv()
    @pl.when(z > 1)
    def _():
        pl.delay(HOLD)
    for i in range(1, nz - 1):
        @pl.when(z > i)
        def _():
            send(i).start()
    @pl.when(cd == 0)
    def _():
        pl.semaphore_wait(cready, cds - 1)
        for i in range(1, cds):
            signal(cgo, "cd", i)

    load_a.wait()
    hi, lo = split(a[...])
    for k in range(nz):
        c = slice(k * width, (k + 1) * width)
        a_cat[k] = jnp.concatenate([hi[:, c], lo[:, c], hi[:, c]], axis=1)

    def product(chip):
        stripes = []
        for i in range(CORES):
            k = chip * CORES + i
            t = tiles[k]
            g = cd * pairs + k
            stripes.append(jnp.concatenate(
                [t * flags[m, g].astype(jnp.float32) for m in range(blocks)], axis=0))
        b_hi, b_lo = split(jnp.concatenate(stripes, axis=1))
        return lax.dot_general(
            a_cat[chip], jnp.concatenate([b_hi, b_hi, b_lo], axis=1),
            dimension_numbers=(((1,), (1,)), ((), ())), preferred_element_type=jnp.float32)

    def source(j):
        return jnp.where(j <= z, z - j, j)

    def add(chip):
        exchange(chip, 1 - core).wait_recv()
        acc[...] += product(chip)

    acc[...] = product(z)

    def gather(j, carry):
        chip = source(j)
        arrival(chip).wait_recv()
        exchange(chip, core).start()
        @pl.when(core == 0)
        def _():
            add(chip)
        return carry

    def rest(j, carry):
        add(source(j))
        return carry

    lax.fori_loop(1, nz, gather, 0)
    @pl.when(core == 1)
    def _():
        lax.fori_loop(1, nz, rest, 0)

    def peer(j):
        return j + jnp.where(j >= cd, 1, 0)

    def scatter(j):
        q = peer(j)
        return pltpu.make_async_remote_copy(
            src_ref=acc.at[pl.ds(pl.multiple_of(q * rows, rows), rows)], dst_ref=land.at[cd],
            send_sem=rs_send.at[q], recv_sem=rs_recv.at[cd],
            device_id={"cd": q}, device_id_type=MESH)

    def landed(q):
        return pltpu.make_async_remote_copy(
            src_ref=acc.at[pl.ds(0, rows)], dst_ref=land.at[q], send_sem=rs_send.at[q], recv_sem=rs_recv.at[q],
            device_id={"cd": q}, device_id_type=MESH)

    @pl.when(cd > 0)
    def _():
        pl.semaphore_wait(cgo, 1)
    for j in range(cds - 1):
        scatter(j).start()

    def drain(j, carry):
        exchange(source(j), core).wait_send()
        send(source(j)).wait_send()
        return carry

    exchange(z, core).wait_send()
    lax.fori_loop(1, nz, drain, 0)

    total = acc[pl.ds(pl.multiple_of(cd * rows, rows), rows)]
    for j in range(cds - 1):
        q = peer(j)
        landed(q).wait_recv()
        total = total + land[q]
    out_ref[...] = total
    for j in range(cds - 1):
        scatter(j).wait_send()


def solution(mesh):
    pairs, cds = mesh.shape["pair"], mesh.shape["cd"]
    nz = pairs // CORES

    def local(amplitudes, integrals, keep_tiles):
        n, depth = amplitudes.shape
        ab = integrals.shape[1]
        rows = n // cds
        return pl.pallas_call(
            functools.partial(kernel, pairs, cds),
            out_shape=pltpu.VMEM((rows, ab), jnp.float32),
            in_specs=[
                pl.BlockSpec(memory_space=pl.ANY),
                pl.BlockSpec(memory_space=pl.ANY),
                pl.BlockSpec(memory_space=pl.ANY),
            ],
            out_specs=pl.BlockSpec(memory_space=pltpu.VMEM),
            scratch_shapes=[
                pltpu.SMEM(keep_tiles.shape[::-1], jnp.int32),
                pltpu.VMEM(integrals.shape, jnp.float32),
                pltpu.VMEM((n, depth), jnp.float32),
                pltpu.VMEM((pairs, TILE, TILE), jnp.float32),
                pltpu.VMEM((nz, n, 3 * CORES * TILE), jnp.bfloat16),
                pltpu.VMEM((n, ab), jnp.float32),
                pltpu.VMEM((cds, rows, ab), jnp.float32),
                pltpu.SemaphoreType.DMA((3,)),
                pltpu.SemaphoreType.DMA((nz,)),
                pltpu.SemaphoreType.DMA((nz,)),
                pltpu.SemaphoreType.DMA((nz,)),
                pltpu.SemaphoreType.DMA((nz,)),
                pltpu.SemaphoreType.DMA((cds,)),
                pltpu.SemaphoreType.DMA((cds,)),
                pltpu.SemaphoreType.REGULAR((nz,)),
                pltpu.SemaphoreType.REGULAR,
                pltpu.SemaphoreType.REGULAR,
                pltpu.SemaphoreType.REGULAR,
            ],
            compiler_params=pltpu.CompilerParams(collective_id=0, has_side_effects=True),
        )(keep_tiles.T, integrals, amplitudes)

    placed = (P("pair", "cd"), P(("cd", "pair"), None), P())
    return jax.shard_map(
        local, mesh=mesh, in_specs=placed, out_specs=P(("pair", "cd"), None), check_vma=False
    )
```

time: 19.2 us -> 17.3 us (0.901)
  the two profiles are of different devices: /device:TPU:0 before, /device:TPU:11 now
where the time goes in v1:
time: 17.3 us; the launch traced here: 17.2 us
  Pallas kernels  16.5 us (95%)
  local copies, waits for them, and re-layouts  0.63 us (4%)
    pallas_call x1, Pallas kernels, local(): pl.pallas_call(functools.partial(kernel, pairs, cds), out_shape=pltpu.VME...  16.5 us
    unnamed x1, local copies, waits for them, and re-layouts  0.63 us

profile of v1, /device:TPU:11, one launch (start us, length us, event | category | flops | bytes accessed | tf_op | source)
XLA Modules:
  0.0 17.2 jit_solution(1031002108165473041)
XLA Ops:
  0.0 16.5 %shard_map.37 = f32[64,256]{1,0:T(8,128)S(1)} custom-call(s32[2,32]{1,0:T(2,128)} %bitcast.1, f32[128,256]{1,0:T(8,128)} %v_hbm.1, f32[256,1024]{1,0:T(8,128)} %a_hbm.1), custom_call_target="tpu_custom_call" | custom-call | tf_op jit(solution)/shard_map/pallas_call | solution.py:215
  16.5 0.6 %copy.5 = f32[64,256]{1,0:T(8,128)} copy(f32[64,256]{1,0:T(8,128)S(1)} %shard_map.37) | data formatting | bytes 131072

commit v2 on v1

--- a/solution.py
+++ b/solution.py
@@ -9,7 +9,7 @@
 
 TILE = 128
 CORES = 2
-HOLD = 1000
+HOLDS = (1000, 700)
 MESH = pl.DeviceIdType.MESH
 
 
@@ -20,7 +20,7 @@
 
 
 def kernel(pairs, cds, flags_hbm, v_hbm, a_hbm, out_ref, flags, v, a, tiles, a_cat, acc, land,
-           load_sem, ssem, rsem, psend, precv, rs_send, rs_recv, zready, pready, cready, cgo):
+           load_sem, ssem, rsem, psend, precv, rs_send, rs_recv, zready, pready, cready, cgo, relay_sem):
     nz = pairs // CORES
     width = CORES * TILE
     me = lax.axis_index("pair")
@@ -36,7 +36,6 @@
     load_f = pltpu.make_async_copy(flags_hbm, flags, load_sem.at[2])
     load_f.start()
     load_a = pltpu.make_async_copy(a_hbm, a, load_sem.at[1])
-    load_a.start()
 
     def signal(sem, axis, to):
         pl.semaphore_signal(sem, inc=1, device_id={axis: to}, device_id_type=MESH)
@@ -74,7 +73,7 @@
     own = v[:, :TILE] * flags[0, row_block].astype(jnp.float32)
     for m in range(1, blocks):
         own = own + v[:, m * TILE:(m + 1) * TILE] * flags[m, row_block].astype(jnp.float32)
-    tiles[me] = own.T
+    tiles[me] = own
 
     def send(chip):
         return pltpu.make_async_remote_copy(
@@ -87,15 +86,26 @@
             src_ref=tiles.at[k], dst_ref=tiles.at[k], send_sem=ssem.at[chip], recv_sem=rsem.at[chip],
             device_id={"pair": k}, device_id_type=MESH)
 
+    def relay(to):
+        k = 2 * CORES + 1
+        return pltpu.make_async_remote_copy(
+            src_ref=tiles.at[k], dst_ref=tiles.at[k], send_sem=relay_sem.at[to],
+            recv_sem=rsem.at[2] if to else precv.at[2], device_id={"pair": to}, device_id_type=MESH)
+
     def exchange(chip, side):
         k = chip * CORES + side
         return pltpu.make_async_remote_copy(
             src_ref=tiles.at[k], dst_ref=tiles.at[k], send_sem=psend.at[chip], recv_sem=precv.at[chip],
             device_id={"pair": partner}, device_id_type=MESH)
 
-    @pl.when(z > 0)
+    relayed = (z == 2) & (core == 1)
+    @pl.when(relayed)
+    def _():
+        send(1).start()
+    @pl.when((z > 0) & jnp.logical_not(relayed))
     def _():
         send(0).start()
+    load_a.start()
     @pl.when(core == 1)
     def _():
         pl.semaphore_wait(pready, 1)
@@ -106,13 +116,14 @@
             pl.semaphore_wait(zready.at[z + i], 1)
             send(z + i).start()
     exchange(z, 1 - core).wait_recv()
-    @pl.when(z > 1)
-    def _():
-        pl.delay(HOLD)
-    for i in range(1, nz - 1):
-        @pl.when(z > i)
-        def _():
-            send(i).start()
+    for side, hold in enumerate(HOLDS):
+        @pl.when((z > 1) & (core == side) & jnp.logical_not(relayed))
+        def _():
+            pl.delay(hold)
+            for i in range(1, nz - 1):
+                @pl.when(z > i)
+                def _():
+                    send(i).start()
     @pl.when(cd == 0)
     def _():
         pl.semaphore_wait(cready, cds - 1)
@@ -132,14 +143,20 @@
             t = tiles[k]
             g = cd * pairs + k
             stripes.append(jnp.concatenate(
-                [t * flags[m, g].astype(jnp.float32) for m in range(blocks)], axis=0))
-        b_hi, b_lo = split(jnp.concatenate(stripes, axis=1))
+                [t * flags[m, g].astype(jnp.float32) for m in range(blocks)], axis=1))
+        b_hi, b_lo = split(jnp.concatenate(stripes, axis=0))
         return lax.dot_general(
-            a_cat[chip], jnp.concatenate([b_hi, b_hi, b_lo], axis=1),
-            dimension_numbers=(((1,), (1,)), ((), ())), preferred_element_type=jnp.float32)
+            a_cat[chip], jnp.concatenate([b_hi, b_hi, b_lo], axis=0),
+            dimension_numbers=(((1,), (0,)), ((), ())), preferred_element_type=jnp.float32)
+
+    def twice(chip):
+        return (z == 0) & (core == 1) & (chip == 2)
 
     def source(j):
-        return jnp.where(j <= z, z - j, j)
+        chip = jnp.where(j <= z, z - j, j)
+        if nz > 3:
+            chip = jnp.where((z == 0) & (j == 2), 3, jnp.where((z == 0) & (j == 3), 2, chip))
+        return chip
 
     def add(chip):
         exchange(chip, 1 - core).wait_recv()
@@ -149,29 +166,39 @@
 
     def gather(j, carry):
         chip = source(j)
-        arrival(chip).wait_recv()
-        exchange(chip, core).start()
+        receive(chip)
         @pl.when(core == 0)
         def _():
             add(chip)
         return carry
+
+    def receive(chip):
+        arrival(chip).wait_recv()
+        @pl.when((z == 1) & (core == 1) & (chip == 2))
+        def _():
+            for i in range(CORES):
+                relay(i).start()
+        @pl.when(jnp.logical_not(twice(chip)))
+        def _():
+            exchange(chip, core).start()
 
     def rest(j, carry):
         add(source(j))
         return carry
 
-    lax.fori_loop(1, nz, gather, 0)
+    lax.fori_loop(1, nz - 1, gather, 0)
+    last = source(nz - 1)
+    receive(last)
     @pl.when(core == 1)
     def _():
-        lax.fori_loop(1, nz, rest, 0)
+        lax.fori_loop(1, nz - 1, rest, 0)
 
     def peer(j):
         return j + jnp.where(j >= cd, 1, 0)
 
-    def scatter(j):
-        q = peer(j)
-        return pltpu.make_async_remote_copy(
-            src_ref=acc.at[pl.ds(pl.multiple_of(q * rows, rows), rows)], dst_ref=land.at[cd],
+    def scatter(q):
+        return pltpu.make_async_remote_copy(
+            src_ref=acc.at[pl.ds(q * rows, rows)], dst_ref=land.at[cd],
             send_sem=rs_send.at[q], recv_sem=rs_recv.at[cd],
             device_id={"cd": q}, device_id_type=MESH)
 
@@ -183,16 +210,30 @@
     @pl.when(cd > 0)
     def _():
         pl.semaphore_wait(cgo, 1)
-    for j in range(cds - 1):
-        scatter(j).start()
+    exchange(last, 1 - core).wait_recv()
+    prod = product(last)
+    for q in range(cds):
+        r = slice(q * rows, (q + 1) * rows)
+        acc[r] += prod[r]
+        @pl.when(cd != q)
+        def _():
+            scatter(q).start()
 
     def drain(j, carry):
-        exchange(source(j), core).wait_send()
-        send(source(j)).wait_send()
+        @pl.when(jnp.logical_not(twice(source(j))))
+        def _():
+            exchange(source(j), core).wait_send()
+        @pl.when(jnp.logical_not(relayed & (source(j) == 0)))
+        def _():
+            send(source(j)).wait_send()
         return carry
 
     exchange(z, core).wait_send()
     lax.fori_loop(1, nz, drain, 0)
+    @pl.when((z == 1) & (core == 1))
+    def _():
+        for i in range(CORES):
+            relay(i).wait_send()
 
     total = acc[pl.ds(pl.multiple_of(cd * rows, rows), rows)]
     for j in range(cds - 1):
@@ -201,7 +242,7 @@
         total = total + land[q]
     out_ref[...] = total
     for j in range(cds - 1):
-        scatter(j).wait_send()
+        landed(peer(j)).wait_send()
 
 
 def solution(mesh):
@@ -240,6 +281,7 @@
                 pltpu.SemaphoreType.REGULAR,
                 pltpu.SemaphoreType.REGULAR,
                 pltpu.SemaphoreType.REGULAR,
+                pltpu.SemaphoreType.DMA((CORES,)),
             ],
             compiler_params=pltpu.CompilerParams(collective_id=0, has_side_effects=True),
         )(keep_tiles.T, integrals, amplitudes)

time: 17.3 us -> 16.1 us (0.931)
  Pallas kernels: 16.5 us -> 15.3 us
    pallas_call x1, Pallas kernels: 16.5 us -> 15.3 us  [local(): pl.pallas_call(functools.partial(kernel, pairs, cds), out_shape=pltpu.VME...]
where the time goes in v2:
time: 16.1 us; the launch traced here: 15.9 us
  Pallas kernels  15.3 us (95%)
  local copies, waits for them, and re-layouts  0.63 us (4%)
    pallas_call x1, Pallas kernels, local(): pl.pallas_call(functools.partial(kernel, pairs, cds), out_shape=pltpu.VME...  15.3 us
    unnamed x1, local copies, waits for them, and re-layouts  0.63 us

profile of v2, /device:TPU:11, one launch (start us, length us, event | category | flops | bytes accessed | tf_op | source)
XLA Modules:
  0.0 15.9 jit_solution(1698258730187413768)
XLA Ops:
  0.0 15.3 %shard_map.37 = f32[64,256]{1,0:T(8,128)S(1)} custom-call(s32[2,32]{1,0:T(2,128)} %bitcast.1, f32[128,256]{1,0:T(8,128)} %v_hbm.1, f32[256,1024]{1,0:T(8,128)} %a_hbm.1), custom_call_target="tpu_custom_call" | custom-call | tf_op jit(solution)/shard_map/pallas_call | solution.py:256
  15.3 0.6 %copy.5 = f32[64,256]{1,0:T(8,128)} copy(f32[64,256]{1,0:T(8,128)S(1)} %shard_map.37) | data formatting | bytes 131072

commit v3 on v2

--- a/solution.py
+++ b/solution.py
@@ -20,7 +20,7 @@
 
 
 def kernel(pairs, cds, flags_hbm, v_hbm, a_hbm, out_ref, flags, v, a, tiles, a_cat, acc, land,
-           load_sem, ssem, rsem, psend, precv, rs_send, rs_recv, zready, pready, cready, cgo, relay_sem):
+           load_sem, sent, rsem, precv, rs_send, rs_recv, zready, pready, entered, relay_sem):
     nz = pairs // CORES
     width = CORES * TILE
     me = lax.axis_index("pair")
@@ -59,13 +59,13 @@
     for i in range(1, nz):
         @pl.when(z >= i)
         def _():
-            signal(zready.at[z], "pair", me - i * CORES)
+            signal(zready.at[i - 1], "pair", me - i * CORES)
     @pl.when(core == 0)
     def _():
         signal(pready, "pair", partner)
     @pl.when(cd > 0)
     def _():
-        signal(cready, "cd", 0)
+        signal(entered, "cd", 0)
 
     load_f.wait()
     load_v.wait()
@@ -77,25 +77,25 @@
 
     def send(chip):
         return pltpu.make_async_remote_copy(
-            src_ref=tiles.at[me], dst_ref=tiles.at[me], send_sem=ssem.at[chip], recv_sem=rsem.at[z],
+            src_ref=tiles.at[me], dst_ref=tiles.at[me], send_sem=sent, recv_sem=rsem.at[z - jnp.where(z > chip, 1, 0)],
             device_id={"pair": chip * CORES + core}, device_id_type=MESH)
 
     def arrival(chip):
         k = chip * CORES + core
         return pltpu.make_async_remote_copy(
-            src_ref=tiles.at[k], dst_ref=tiles.at[k], send_sem=ssem.at[chip], recv_sem=rsem.at[chip],
+            src_ref=tiles.at[k], dst_ref=tiles.at[k], send_sem=sent, recv_sem=rsem.at[chip - jnp.where(chip > z, 1, 0)],
             device_id={"pair": k}, device_id_type=MESH)
 
     def relay(to):
         k = 2 * CORES + 1
         return pltpu.make_async_remote_copy(
-            src_ref=tiles.at[k], dst_ref=tiles.at[k], send_sem=relay_sem.at[to],
-            recv_sem=rsem.at[2] if to else precv.at[2], device_id={"pair": to}, device_id_type=MESH)
+            src_ref=tiles.at[k], dst_ref=tiles.at[k], send_sem=relay_sem,
+            recv_sem=rsem.at[1] if to else precv.at[2], device_id={"pair": to}, device_id_type=MESH)
 
     def exchange(chip, side):
         k = chip * CORES + side
         return pltpu.make_async_remote_copy(
-            src_ref=tiles.at[k], dst_ref=tiles.at[k], send_sem=psend.at[chip], recv_sem=precv.at[chip],
+            src_ref=tiles.at[k], dst_ref=tiles.at[k], send_sem=sent, recv_sem=precv.at[chip],
             device_id={"pair": partner}, device_id_type=MESH)
 
     relayed = (z == 2) & (core == 1)
@@ -113,7 +113,7 @@
     for i in range(1, nz):
         @pl.when(z + i < nz)
         def _():
-            pl.semaphore_wait(zready.at[z + i], 1)
+            pl.semaphore_wait(zready.at[i - 1], 1)
             send(z + i).start()
     exchange(z, 1 - core).wait_recv()
     for side, hold in enumerate(HOLDS):
@@ -126,9 +126,9 @@
                     send(i).start()
     @pl.when(cd == 0)
     def _():
-        pl.semaphore_wait(cready, cds - 1)
+        pl.semaphore_wait(entered, cds - 1)
         for i in range(1, cds):
-            signal(cgo, "cd", i)
+            signal(entered, "cd", i)
 
     load_a.wait()
     hi, lo = split(a[...])
@@ -193,23 +193,19 @@
     def _():
         lax.fori_loop(1, nz - 1, rest, 0)
 
-    def peer(j):
-        return j + jnp.where(j >= cd, 1, 0)
-
     def scatter(q):
         return pltpu.make_async_remote_copy(
-            src_ref=acc.at[pl.ds(q * rows, rows)], dst_ref=land.at[cd],
-            send_sem=rs_send.at[q], recv_sem=rs_recv.at[cd],
-            device_id={"cd": q}, device_id_type=MESH)
-
-    def landed(q):
-        return pltpu.make_async_remote_copy(
-            src_ref=acc.at[pl.ds(0, rows)], dst_ref=land.at[q], send_sem=rs_send.at[q], recv_sem=rs_recv.at[q],
-            device_id={"cd": q}, device_id_type=MESH)
+            src_ref=acc.at[pl.ds(q * rows, rows)], dst_ref=land.at[cd - jnp.where(cd > q, 1, 0)],
+            send_sem=rs_send, recv_sem=rs_recv, device_id={"cd": q}, device_id_type=MESH)
+
+    def scattered():
+        return pltpu.make_async_remote_copy(
+            src_ref=acc.at[pl.ds(0, (cds - 1) * rows)], dst_ref=land,
+            send_sem=rs_send, recv_sem=rs_recv, device_id={"cd": lax.rem(cd + 1, cds)}, device_id_type=MESH)
 
     @pl.when(cd > 0)
     def _():
-        pl.semaphore_wait(cgo, 1)
+        pl.semaphore_wait(entered, 1)
     exchange(last, 1 - core).wait_recv()
     prod = product(last)
     for q in range(cds):
@@ -219,30 +215,28 @@
         def _():
             scatter(q).start()
 
-    def drain(j, carry):
-        @pl.when(jnp.logical_not(twice(source(j))))
-        def _():
-            exchange(source(j), core).wait_send()
-        @pl.when(jnp.logical_not(relayed & (source(j) == 0)))
-        def _():
-            send(source(j)).wait_send()
-        return carry
-
-    exchange(z, core).wait_send()
-    lax.fori_loop(1, nz, drain, 0)
+    def drained(n, sem):
+        return pltpu.make_async_remote_copy(
+            src_ref=tiles.at[pl.ds(0, n)], dst_ref=tiles.at[pl.ds(0, n)], send_sem=sem, recv_sem=rsem.at[0],
+            device_id={"pair": partner}, device_id_type=MESH)
+
+    fewer = relayed | twice(2)
+    @pl.when(jnp.logical_not(fewer))
+    def _():
+        drained(2 * nz - 1, sent).wait_send()
+    @pl.when(fewer)
+    def _():
+        drained(2 * nz - 2, sent).wait_send()
     @pl.when((z == 1) & (core == 1))
     def _():
-        for i in range(CORES):
-            relay(i).wait_send()
+        drained(CORES, relay_sem).wait_send()
 
     total = acc[pl.ds(pl.multiple_of(cd * rows, rows), rows)]
-    for j in range(cds - 1):
-        q = peer(j)
-        landed(q).wait_recv()
-        total = total + land[q]
+    scattered().wait_recv()
+    for i in range(cds - 1):
+        total = total + land[i]
     out_ref[...] = total
-    for j in range(cds - 1):
-        landed(peer(j)).wait_send()
+    scattered().wait_send()
 
 
 def solution(mesh):
@@ -269,19 +263,17 @@
                 pltpu.VMEM((pairs, TILE, TILE), jnp.float32),
                 pltpu.VMEM((nz, n, 3 * CORES * TILE), jnp.bfloat16),
                 pltpu.VMEM((n, ab), jnp.float32),
-                pltpu.VMEM((cds, rows, ab), jnp.float32),
+                pltpu.VMEM((cds - 1, rows, ab), jnp.float32),
                 pltpu.SemaphoreType.DMA((3,)),
+                pltpu.SemaphoreType.DMA,
+                pltpu.SemaphoreType.DMA((nz - 1,)),
                 pltpu.SemaphoreType.DMA((nz,)),
-                pltpu.SemaphoreType.DMA((nz,)),
-                pltpu.SemaphoreType.DMA((nz,)),
-                pltpu.SemaphoreType.DMA((nz,)),
-                pltpu.SemaphoreType.DMA((cds,)),
-                pltpu.SemaphoreType.DMA((cds,)),
-                pltpu.SemaphoreType.REGULAR((nz,)),
+                pltpu.SemaphoreType.DMA,
+                pltpu.SemaphoreType.DMA,
+                pltpu.SemaphoreType.REGULAR((nz - 1,)),
                 pltpu.SemaphoreType.REGULAR,
                 pltpu.SemaphoreType.REGULAR,
-                pltpu.SemaphoreType.REGULAR,
-                pltpu.SemaphoreType.DMA((CORES,)),
+                pltpu.SemaphoreType.DMA,
             ],
             compiler_params=pltpu.CompilerParams(collective_id=0, has_side_effects=True),
         )(keep_tiles.T, integrals, amplitudes)

time: 16.1 us -> 15.9 us (0.988)
  Pallas kernels: 15.3 us -> 15.1 us
where the time goes in v3:
time: 15.9 us; the launch traced here: 15.8 us
  Pallas kernels  15.1 us (95%)
  local copies, waits for them, and re-layouts  0.63 us (4%)
    pallas_call x1, Pallas kernels, local(): pl.pallas_call(functools.partial(kernel, pairs, cds), out_shape=pltpu.VME...  15.1 us
    unnamed x1, local copies, waits for them, and re-layouts  0.63 us

profile of v3, /device:TPU:11, one launch (start us, length us, event | category | flops | bytes accessed | tf_op | source)
XLA Modules:
  0.0 15.8 jit_solution(16081802445090875327)
XLA Ops:
  0.0 15.1 %shard_map.37 = f32[64,256]{1,0:T(8,128)S(1)} custom-call(s32[2,32]{1,0:T(2,128)} %bitcast.1, f32[128,256]{1,0:T(8,128)} %v_hbm.1, f32[256,1024]{1,0:T(8,128)} %a_hbm.1), custom_call_target="tpu_custom_call" | custom-call | tf_op jit(solution)/shard_map/pallas_call | solution.py:250
  15.1 0.6 %copy.5 = f32[64,256]{1,0:T(8,128)} copy(f32[64,256]{1,0:T(8,128)S(1)} %shard_map.37) | data formatting | bytes 131072

commit v4 on v3

--- a/solution.py
+++ b/solution.py
@@ -20,9 +20,8 @@
 
 
 def kernel(pairs, cds, flags_hbm, v_hbm, a_hbm, out_ref, flags, v, a, tiles, a_cat, acc, land,
-           load_sem, sent, rsem, precv, rs_send, rs_recv, zready, pready, entered, relay_sem):
+           sem, rsem, precv, rs_recv, zready, pready, entered):
     nz = pairs // CORES
-    width = CORES * TILE
     me = lax.axis_index("pair")
     cd = lax.axis_index("cd")
     z = lax.div(me, CORES)
@@ -31,11 +30,11 @@
     blocks = v.shape[1] // TILE
     rows = out_ref.shape[0]
 
-    load_v = pltpu.make_async_copy(v_hbm, v, load_sem.at[0])
+    load_v = pltpu.make_async_copy(v_hbm, v, sem.at[0])
     load_v.start()
-    load_f = pltpu.make_async_copy(flags_hbm, flags, load_sem.at[2])
+    load_f = pltpu.make_async_copy(flags_hbm, flags, sem.at[2])
     load_f.start()
-    load_a = pltpu.make_async_copy(a_hbm, a, load_sem.at[1])
+    load_a = pltpu.make_async_copy(a_hbm, a, sem.at[1])
 
     def signal(sem, axis, to):
         pl.semaphore_signal(sem, inc=1, device_id={axis: to}, device_id_type=MESH)
@@ -77,25 +76,25 @@
 
     def send(chip):
         return pltpu.make_async_remote_copy(
-            src_ref=tiles.at[me], dst_ref=tiles.at[me], send_sem=sent, recv_sem=rsem.at[z - jnp.where(z > chip, 1, 0)],
+            src_ref=tiles.at[me], dst_ref=tiles.at[me], send_sem=sem.at[0], recv_sem=rsem.at[z - jnp.where(z > chip, 1, 0)],
             device_id={"pair": chip * CORES + core}, device_id_type=MESH)
 
     def arrival(chip):
         k = chip * CORES + core
         return pltpu.make_async_remote_copy(
-            src_ref=tiles.at[k], dst_ref=tiles.at[k], send_sem=sent, recv_sem=rsem.at[chip - jnp.where(chip > z, 1, 0)],
+            src_ref=tiles.at[k], dst_ref=tiles.at[k], send_sem=sem.at[0], recv_sem=rsem.at[chip - jnp.where(chip > z, 1, 0)],
             device_id={"pair": k}, device_id_type=MESH)
 
     def relay(to):
         k = 2 * CORES + 1
         return pltpu.make_async_remote_copy(
-            src_ref=tiles.at[k], dst_ref=tiles.at[k], send_sem=relay_sem,
+            src_ref=tiles.at[k], dst_ref=tiles.at[k], send_sem=sem.at[1],
             recv_sem=rsem.at[1] if to else precv.at[2], device_id={"pair": to}, device_id_type=MESH)
 
     def exchange(chip, side):
         k = chip * CORES + side
         return pltpu.make_async_remote_copy(
-            src_ref=tiles.at[k], dst_ref=tiles.at[k], send_sem=sent, recv_sem=precv.at[chip],
+            src_ref=tiles.at[k], dst_ref=tiles.at[k], send_sem=sem.at[0], recv_sem=precv.at[chip],
             device_id={"pair": partner}, device_id_type=MESH)
 
     relayed = (z == 2) & (core == 1)
@@ -132,6 +131,7 @@
 
     load_a.wait()
     hi, lo = split(a[...])
+    width = CORES * TILE
     for k in range(nz):
         c = slice(k * width, (k + 1) * width)
         a_cat[k] = jnp.concatenate([hi[:, c], lo[:, c], hi[:, c]], axis=1)
@@ -139,25 +139,39 @@
     def product(chip):
         stripes = []
         for i in range(CORES):
-            k = chip * CORES + i
-            t = tiles[k]
-            g = cd * pairs + k
+            t = tiles[chip * CORES + i]
+            g = cd * pairs + chip * CORES + i
             stripes.append(jnp.concatenate(
                 [t * flags[m, g].astype(jnp.float32) for m in range(blocks)], axis=1))
         b_hi, b_lo = split(jnp.concatenate(stripes, axis=0))
-        return lax.dot_general(
-            a_cat[chip], jnp.concatenate([b_hi, b_hi, b_lo], axis=0),
-            dimension_numbers=(((1,), (0,)), ((), ())), preferred_element_type=jnp.float32)
-
-    def twice(chip):
-        return (z == 0) & (core == 1) & (chip == 2)
+        return jnp.dot(
+            a_cat[chip], jnp.concatenate([b_hi, b_hi, b_lo], axis=0), preferred_element_type=jnp.float32)
+
+    def plain(j):
+        return jnp.where(j <= z, z - j, j)
 
     def source(j):
-        chip = jnp.where(j <= z, z - j, j)
+        chip = plain(j)
         if nz > 3:
             chip = jnp.where((z == 0) & (j == 2), 3, jnp.where((z == 0) & (j == 3), 2, chip))
         return chip
 
+    last = jnp.where(core == 0, source(nz - 1), plain(nz - 1))
+    by_relay = (z == 0) & (core == 0) & (last == 2)
+
+    def twice(chip):
+        return (z == 0) & (core == 1) & (chip == 2)
+
+    def receive(chip):
+        arrival(chip).wait_recv()
+        @pl.when((z == 1) & (core == 1) & (chip == 2))
+        def _():
+            for i in range(CORES):
+                relay(i).start()
+        @pl.when(jnp.logical_not(twice(chip)))
+        def _():
+            exchange(chip, core).start()
+
     def add(chip):
         exchange(chip, 1 - core).wait_recv()
         acc[...] += product(chip)
@@ -165,30 +179,23 @@
     acc[...] = product(z)
 
     def gather(j, carry):
-        chip = source(j)
-        receive(chip)
+        @pl.when(by_relay & (j == 2))
+        def _():
+            receive(last)
+        receive(source(j))
         @pl.when(core == 0)
         def _():
-            add(chip)
+            add(source(j))
         return carry
 
-    def receive(chip):
-        arrival(chip).wait_recv()
-        @pl.when((z == 1) & (core == 1) & (chip == 2))
-        def _():
-            for i in range(CORES):
-                relay(i).start()
-        @pl.when(jnp.logical_not(twice(chip)))
-        def _():
-            exchange(chip, core).start()
-
     def rest(j, carry):
-        add(source(j))
+        add(plain(j))
         return carry
 
     lax.fori_loop(1, nz - 1, gather, 0)
-    last = source(nz - 1)
-    receive(last)
+    @pl.when((core == 1) | jnp.logical_not(by_relay))
+    def _():
+        receive(source(nz - 1))
     @pl.when(core == 1)
     def _():
         lax.fori_loop(1, nz - 1, rest, 0)
@@ -196,12 +203,12 @@
     def scatter(q):
         return pltpu.make_async_remote_copy(
             src_ref=acc.at[pl.ds(q * rows, rows)], dst_ref=land.at[cd - jnp.where(cd > q, 1, 0)],
-            send_sem=rs_send, recv_sem=rs_recv, device_id={"cd": q}, device_id_type=MESH)
+            send_sem=sem.at[2], recv_sem=rs_recv, device_id={"cd": q}, device_id_type=MESH)
 
     def scattered():
         return pltpu.make_async_remote_copy(
             src_ref=acc.at[pl.ds(0, (cds - 1) * rows)], dst_ref=land,
-            send_sem=rs_send, recv_sem=rs_recv, device_id={"cd": lax.rem(cd + 1, cds)}, device_id_type=MESH)
+            send_sem=sem.at[2], recv_sem=rs_recv, device_id={"cd": lax.rem(cd + 1, cds)}, device_id_type=MESH)
 
     @pl.when(cd > 0)
     def _():
@@ -223,13 +230,13 @@
     fewer = relayed | twice(2)
     @pl.when(jnp.logical_not(fewer))
     def _():
-        drained(2 * nz - 1, sent).wait_send()
+        drained(2 * nz - 1, sem.at[0]).wait_send()
     @pl.when(fewer)
     def _():
-        drained(2 * nz - 2, sent).wait_send()
+        drained(2 * nz - 2, sem.at[0]).wait_send()
     @pl.when((z == 1) & (core == 1))
     def _():
-        drained(CORES, relay_sem).wait_send()
+        drained(CORES, sem.at[1]).wait_send()
 
     total = acc[pl.ds(pl.multiple_of(cd * rows, rows), rows)]
     scattered().wait_recv()
@@ -265,15 +272,12 @@
                 pltpu.VMEM((n, ab), jnp.float32),
                 pltpu.VMEM((cds - 1, rows, ab), jnp.float32),
                 pltpu.SemaphoreType.DMA((3,)),
-                pltpu.SemaphoreType.DMA,
                 pltpu.SemaphoreType.DMA((nz - 1,)),
                 pltpu.SemaphoreType.DMA((nz,)),
-                pltpu.SemaphoreType.DMA,
                 pltpu.SemaphoreType.DMA,
                 pltpu.SemaphoreType.REGULAR((nz - 1,)),
                 pltpu.SemaphoreType.REGULAR,
                 pltpu.SemaphoreType.REGULAR,
-                pltpu.SemaphoreType.DMA,
             ],
             compiler_params=pltpu.CompilerParams(collective_id=0, has_side_effects=True),
         )(keep_tiles.T, integrals, amplitudes)

time: 15.9 us -> 15.9 us (level)
  no operation moved by 1% of the time
where the time goes in v4:
time: 15.9 us; the launch traced here: 15.7 us
  Pallas kernels  15.1 us (95%)
  local copies, waits for them, and re-layouts  0.63 us (4%)
    pallas_call x1, Pallas kernels, local(): pl.pallas_call(functools.partial(kernel, pairs, cds), out_shape=pltpu.VME...  15.1 us
    unnamed x1, local copies, waits for them, and re-layouts  0.63 us

profile of v4, /device:TPU:11, one launch (start us, length us, event | category | flops | bytes accessed | tf_op | source)
XLA Modules:
  0.0 15.7 jit_solution(8980054446094910436)
XLA Ops:
  0.0 15.1 %shard_map.37 = f32[64,256]{1,0:T(8,128)S(1)} custom-call(s32[2,32]{1,0:T(2,128)} %bitcast.1, f32[128,256]{1,0:T(8,128)} %v_hbm.1, f32[256,1024]{1,0:T(8,128)} %a_hbm.1), custom_call_target="tpu_custom_call" | custom-call | tf_op jit(solution)/shard_map/pallas_call | solution.py:257
  15.1 0.6 %copy.5 = f32[64,256]{1,0:T(8,128)} copy(f32[64,256]{1,0:T(8,128)S(1)} %shard_map.37) | data formatting | bytes 131072

commit v5 on v4

--- a/solution.py
+++ b/solution.py
@@ -10,6 +10,7 @@
 TILE = 128
 CORES = 2
 HOLDS = (1000, 700)
+HOLD_SUMS = 600
 MESH = pl.DeviceIdType.MESH
 
 
@@ -215,12 +216,17 @@
         pl.semaphore_wait(entered, 1)
     exchange(last, 1 - core).wait_recv()
     prod = product(last)
+    held = cd == 2
     for q in range(cds):
         r = slice(q * rows, (q + 1) * rows)
         acc[r] += prod[r]
-        @pl.when(cd != q)
+        @pl.when((cd != q) & jnp.logical_not(held) if q == 1 else cd != q)
         def _():
             scatter(q).start()
+    @pl.when(held)
+    def _():
+        pl.delay(HOLD_SUMS)
+        scatter(1).start()
 
     def drained(n, sem):
         return pltpu.make_async_remote_copy(

time: 15.9 us -> 15.7 us (0.987)
  Pallas kernels: 15.1 us -> 14.9 us
    pallas_call x1, Pallas kernels: 15.1 us -> 14.9 us  [local(): pl.pallas_call(functools.partial(kernel, pairs, cds), out_shape=pltpu.VME...]
where the time goes in v5:
time: 15.7 us; the launch traced here: 15.5 us
  Pallas kernels  14.9 us (95%)
  local copies, waits for them, and re-layouts  0.63 us (4%)
    pallas_call x1, Pallas kernels, local(): pl.pallas_call(functools.partial(kernel, pairs, cds), out_shape=pltpu.VME...  14.9 us
    unnamed x1, local copies, waits for them, and re-layouts  0.63 us

profile of v5, /device:TPU:11, one launch (start us, length us, event | category | flops | bytes accessed | tf_op | source)
XLA Modules:
  0.0 15.5 jit_solution(10451733451866444062)
XLA Ops:
  0.0 14.9 %shard_map.37 = f32[64,256]{1,0:T(8,128)S(1)} custom-call(s32[2,32]{1,0:T(2,128)} %bitcast.1, f32[128,256]{1,0:T(8,128)} %v_hbm.1, f32[256,1024]{1,0:T(8,128)} %a_hbm.1), custom_call_target="tpu_custom_call" | custom-call | tf_op jit(solution)/shard_map/pallas_call | solution.py:263
  14.9 0.6 %copy.5 = f32[64,256]{1,0:T(8,128)} copy(f32[64,256]{1,0:T(8,128)S(1)} %shard_map.37) | data formatting | bytes 131072

commit v6 on v5

--- a/solution.py
+++ b/solution.py
@@ -137,16 +137,22 @@
         c = slice(k * width, (k + 1) * width)
         a_cat[k] = jnp.concatenate([hi[:, c], lo[:, c], hi[:, c]], axis=1)
 
-    def product(chip):
+    def operands(chip, sides):
         stripes = []
-        for i in range(CORES):
+        for i in sides:
             t = tiles[chip * CORES + i]
             g = cd * pairs + chip * CORES + i
             stripes.append(jnp.concatenate(
                 [t * flags[m, g].astype(jnp.float32) for m in range(blocks)], axis=1))
         b_hi, b_lo = split(jnp.concatenate(stripes, axis=0))
+        lo, hi = sides[0] * TILE, (sides[-1] + 1) * TILE
+        left = [a_cat[chip, :, part * width + lo:part * width + hi] for part in range(3)]
+        return left, [b_hi, b_hi, b_lo]
+
+    def product(*terms):
+        left, right = (sum(t, []) for t in zip(*(operands(*term) for term in terms)))
         return jnp.dot(
-            a_cat[chip], jnp.concatenate([b_hi, b_hi, b_lo], axis=0), preferred_element_type=jnp.float32)
+            jnp.concatenate(left, axis=1), jnp.concatenate(right, axis=0), preferred_element_type=jnp.float32)
 
     def plain(j):
         return jnp.where(j <= z, z - j, j)
@@ -175,9 +181,9 @@
 
     def add(chip):
         exchange(chip, 1 - core).wait_recv()
-        acc[...] += product(chip)
-
-    acc[...] = product(z)
+        acc[...] += product((chip, (0, 1)))
+
+    acc[...] = product((z, (0, 1)))
 
     def gather(j, carry):
         @pl.when(by_relay & (j == 2))
@@ -199,7 +205,10 @@
         receive(source(nz - 1))
     @pl.when(core == 1)
     def _():
-        lax.fori_loop(1, nz - 1, rest, 0)
+        lax.fori_loop(1, nz - 2, rest, 0)
+        before = plain(nz - 2)
+        exchange(before, 0).wait_recv()
+        acc[...] += product((before, (0, 1)), (last, (1,)))
 
     def scatter(q):
         return pltpu.make_async_remote_copy(
@@ -214,15 +223,21 @@
     @pl.when(cd > 0)
     def _():
         pl.semaphore_wait(entered, 1)
+    held = cd == 2
+
+    def finish(prod):
+        for q in range(cds):
+            r = slice(q * rows, (q + 1) * rows)
+            acc[r] += prod[r]
+            @pl.when((cd != q) & jnp.logical_not(held) if q == 1 else cd != q)
+            def _():
+                scatter(q).start()
+
     exchange(last, 1 - core).wait_recv()
-    prod = product(last)
-    held = cd == 2
-    for q in range(cds):
-        r = slice(q * rows, (q + 1) * rows)
-        acc[r] += prod[r]
-        @pl.when((cd != q) & jnp.logical_not(held) if q == 1 else cd != q)
-        def _():
-            scatter(q).start()
+    for side, tail in enumerate(((0, 1), (0,))):
+        @pl.when(core == side)
+        def _():
+            finish(product((last, tail)))
     @pl.when(held)
     def _():
         pl.delay(HOLD_SUMS)

time: 15.7 us -> 15.8 us (level)
  no operation moved by 1% of the time
where the time goes in v6:
time: 15.8 us; the launch traced here: 15.5 us
  Pallas kernels  14.9 us (94%)
  local copies, waits for them, and re-layouts  0.63 us (4%)
    pallas_call x1, Pallas kernels, local(): pl.pallas_call(functools.partial(kernel, pairs, cds), out_shape=pltpu.VME...  14.9 us
    unnamed x1, local copies, waits for them, and re-layouts  0.63 us

profile of v6, /device:TPU:11, one launch (start us, length us, event | category | flops | bytes accessed | tf_op | source)
XLA Modules:
  0.0 15.5 jit_solution(3139164276697831536)
XLA Ops:
  0.0 14.9 %shard_map.37 = f32[64,256]{1,0:T(8,128)S(1)} custom-call(s32[2,32]{1,0:T(2,128)} %bitcast.1, f32[128,256]{1,0:T(8,128)} %v_hbm.1, f32[256,1024]{1,0:T(8,128)} %a_hbm.1), custom_call_target="tpu_custom_call" | custom-call | tf_op jit(solution)/shard_map/pallas_call | solution.py:278
  14.9 0.6 %copy.5 = f32[64,256]{1,0:T(8,128)} copy(f32[64,256]{1,0:T(8,128)S(1)} %shard_map.37) | data formatting | bytes 131072

commit v7 on v5

--- a/solution.py
+++ b/solution.py
@@ -9,8 +9,8 @@
 
 TILE = 128
 CORES = 2
-HOLDS = (1000, 700)
-HOLD_SUMS = 600
+HOLDS = (950, 600)
+HOLD_SUMS = 450
 MESH = pl.DeviceIdType.MESH
 
 

time: 15.7 us -> 15.7 us (level)
  no operation moved by 1% of the time
where the time goes in v7:
time: 15.7 us; the launch traced here: 15.5 us
  Pallas kernels  14.8 us (94%)
  local copies, waits for them, and re-layouts  0.63 us (4%)
    pallas_call x1, Pallas kernels, local(): pl.pallas_call(functools.partial(kernel, pairs, cds), out_shape=pltpu.VME...  14.8 us
    unnamed x1, local copies, waits for them, and re-layouts  0.63 us

profile of v7, /device:TPU:11, one launch (start us, length us, event | category | flops | bytes accessed | tf_op | source)
XLA Modules:
  0.0 15.5 jit_solution(4275016583331881229)
XLA Ops:
  0.0 14.8 %shard_map.37 = f32[64,256]{1,0:T(8,128)S(1)} custom-call(s32[2,32]{1,0:T(2,128)} %bitcast.1, f32[128,256]{1,0:T(8,128)} %v_hbm.1, f32[256,1024]{1,0:T(8,128)} %a_hbm.1), custom_call_target="tpu_custom_call" | custom-call | tf_op jit(solution)/shard_map/pallas_call | solution.py:263
  14.8 0.6 %copy.5 = f32[64,256]{1,0:T(8,128)} copy(f32[64,256]{1,0:T(8,128)S(1)} %shard_map.37) | data formatting | bytes 131072
